TPU v7x, 512 devices: a whole 4x8x8 slice. The times are simulated.
512 devices in a mesh: ta: 8 (over y), gz: 8 (over x, core), xy: 8 (over z).
Axes of the slice: x: 4, y: 8, z: 8, core: 2. Of those that a mesh axis runs over, the one named last changes fastest.
Arguments:
- right_side: float32 [8, 8, 8, 2, 32, 128], P('ta', 'gz', 'xy'), may hold values from -40 to 40
- stencil: float32 [8, 8, 8, 2, 9, 128, 128], P('ta', 'gz', 'xy'), may hold values from -0.5 to 1.5, as said below
- restrict: float32 [8, 8, 8, 2, 32, 128], P('ta', 'gz', 'xy'), may hold values from -0.5 to 0.5
- aggregate: int32 [8, 8, 8, 2], P('ta', 'gz', 'xy'), may hold values from 0 to 63, as said below
- coarsest_inverse: float32 [2048, 2048], P('xy'), may hold values from -0.125 to 0.125
Outputs:
- solution: float32 [8, 8, 8, 2, 32, 128], P('ta', 'gz', 'xy')
- residual: float32 [8, 8, 8, 2, 32, 128], P('ta', 'gz', 'xy')
Inputs may be any that keep to these rules, and one draw needn't show every extreme that they name: `aggregate`: sites are grouped into 2 x 2 x 2 x 2 blocks aligned at even coordinates; each block forms one coarsest site, and the coarsest sites are numbered in an order drawn from the seed. `stencil`: each self block is close to the identity; the other blocks are small and full.
All inputs are finite; a program needn't handle non-finite values.
Results may differ from a plain program's by a relative error of at most 0.0001.
Values sent between devices are 32-bit elements; how exact they have to be, the bound alone decides.
No kernel may reach another device: no remote copies, remote signals or barrier semaphores. Data moves between devices by JAX's collectives and lax.ppermute only.
A program may use at most 64 MiB of HBM per device.

v0:
```python
import jax
import jax.numpy as jnp
from jax import lax
from jax.sharding import PartitionSpec as P


def extended(cells, sides, width):
    for axis, dim in sides:
        count = lax.axis_size(axis)
        head = lax.slice_in_dim(cells, 0, width, axis=dim)
        tail = lax.slice_in_dim(cells, cells.shape[dim] - width, cells.shape[dim], axis=dim)
        cells = jnp.concatenate(
            [
                lax.ppermute(tail, axis, [(i, (i + 1) % count) for i in range(count)]),
                cells,
                lax.ppermute(head, axis, [((i + 1) % count, i) for i in range(count)]),
            ],
            axis=dim,
        )
    return cells


def apply_operator(field, stencil):
    padded = extended(field, (("ta", 0), ("gz", 1), ("xy", 2)), 1)
    centre = field[0, 0, 0]
    stacked = jnp.stack(
        [
            centre,
            padded[2, 1, 1],
            padded[0, 1, 1],
            padded[1, 2, 1],
            padded[1, 0, 1],
            padded[1, 1, 2],
            padded[1, 1, 0],
            jnp.roll(centre, -1, 0),
            jnp.roll(centre, 1, 0),
        ],
        axis=1,
    )
    result = jnp.einsum(
        "xkij,xkrj->xri", stencil[0, 0, 0], stacked, precision=lax.Precision.HIGHEST
    )
    return result[None, None, None]


def inner_sum(one_side, other_side):
    return jnp.sum(one_side * other_side, axis=(0, 1, 2, 3, 5))


def body(right_side, stencil, restrict, aggregate, coarsest_inverse):
    image_first = apply_operator(right_side, stencil)
    cross_first, square_first = lax.psum(
        (inner_sum(image_first, right_side), inner_sum(image_first, image_first)),
        ("ta", "gz", "xy"),
    )
    step_first = cross_first / square_first
    resid_mid = right_side - step_first[:, None] * image_first
    image_raw = apply_operator(resid_mid, stencil)
    correlation_sum = lax.psum(inner_sum(image_first, image_raw), ("ta", "gz", "xy"))
    beta = correlation_sum / square_first
    image_second = image_raw - beta[:, None] * image_first
    direction = resid_mid - beta[:, None] * right_side
    cross_second, square_second = lax.psum(
        (inner_sum(image_second, resid_mid), inner_sum(image_second, image_second)),
        ("ta", "gz", "xy"),
    )
    step_second = cross_second / square_second
    solution_gcr = step_first[:, None] * right_side + step_second[:, None] * direction
    residual = resid_mid - step_second[:, None] * image_second
    vectors = restrict[0, 0, 0]
    comps = vectors.shape[1]
    aggregates = coarsest_inverse.shape[1] // comps
    nrhs_count = residual.shape[4]
    restricted = jnp.einsum(
        "xkc,xrc->xrk", vectors, residual[0, 0, 0], precision=lax.Precision.HIGHEST
    )
    labels = aggregate[0, 0, 0]
    onehot = (labels[:, None] == jnp.arange(aggregates, dtype=jnp.int32)[None, :]).astype(
        jnp.float32
    )
    partial_rhs = jnp.einsum("xa,xrk->akr", onehot, restricted, precision=lax.Precision.HIGHEST)
    partial_rhs = partial_rhs.reshape(aggregates * comps, nrhs_count)
    coarse_rhs = lax.psum(partial_rhs, ("ta", "gz", "xy"))
    rows_part = jnp.dot(
        coarsest_inverse,
        coarse_rhs,
        precision=lax.Precision.HIGHEST,
        preferred_element_type=jnp.float32,
    )
    correction = lax.all_gather(rows_part, "xy", axis=0, tiled=True)
    correction = correction.reshape(aggregates, comps, nrhs_count)
    per_site = jnp.einsum("xa,akr->xkr", onehot, correction, precision=lax.Precision.HIGHEST)
    lifted = jnp.einsum("xkc,xkr->xrc", vectors, per_site, precision=lax.Precision.HIGHEST)
    solution = solution_gcr + lifted[None, None, None]
    return (solution, residual)


def solution(mesh):
    return jax.shard_map(
        body,
        mesh=mesh,
        in_specs=(
            P("ta", "gz", "xy", None, None, None),
            P("ta", "gz", "xy", None, None, None, None),
            P("ta", "gz", "xy", None, None, None),
            P("ta", "gz", "xy", None),
            P("xy", None),
        ),
        out_specs=(P("ta", "gz", "xy", None, None, None), P("ta", "gz", "xy", None, None, None)),
        check_vma=False,
    )
```

profile of v0, /device:TPU:26, one launch (start us, length us, event | category | flops | bytes accessed | tf_op | source)
XLA Modules:
  0.0 679.4 jit_solution(10552285033728135520)
XLA Ops:
  7.2 0.0 copy-start
  7.2 0.0 copy-start.2
  7.2 0.0 copy-start.1
  7.2 0.0 all-reduce.4.cloned.1.call-start
  7.2 5.0 collective-permute-start.1
  12.2 1.9 collective-permute-start
  14.1 0.8 constant_dynamic-update-slice_fusion.11
  14.9 0.7 slice_bitcast_fusion.11
  15.7 0.0 collective-permute-done.1
  15.7 0.8 constant_dynamic-update-slice_fusion.1
  16.4 3.0 collective-permute-done
  19.5 0.0 collective-permute-start.3
  19.5 1.7 collective-permute-start.2
  21.2 2.3 collective-permute-done.3
  23.5 0.0 collective-permute-done.2
  23.5 4.3 collective-permute-start.5
  27.8 8.6 %collective-permute-start.4 = (f32[3,3,1,2,32,128]{5,4,3,2,1,0:T(8,128)S(1)}, f32[3,3,1,2,32,128]{5,4,3,2,1,0:T(8,128)S(1)}, u32[]{:S(2)}, u32[]{:S(2)}) collective-permute-start(f32[3,3,1,2,32,128]{5,4,3,2,1,0:T(8,128)S(1)} %pad_maximum_fusion), channel_id=1, source_target_pairs={{1,0},{2,1},{3,2},{4,3},{5,4},{6,5},{7,6},{0,7},{9,8},{10,9},{11,1... | collective-permute-start | bytes 884744 | tf_op jit(solution)/shard_map/ppermute | solution.py:16
  36.4 6.7 collective-permute-done.4
  43.2 0.0 collective-permute-done.5
  43.2 0.0 copy-done.2
  43.2 0.0 copy-done.1
  43.2 1.4 fusion.6
  44.6 0.1 fusion.13
  44.8 97.5 %all-reduce.1 = (f32[32]{0:T(128)S(1)}, f32[32]{0:T(128)S(1)}) all-reduce(f32[32]{0:T(128)S(1)} %get-tuple-element.14, f32[32]{0:T(128)S(1)} %fusion.13), channel_id=1, replica_groups=mesh['ta'=8,'gz'=8,'xy'=8] {'ta','gz','xy'}, use_global_device_ids=true, to_apply=%region_1.2 | all-reduce | flops 64 | bytes 512 | tf_op jit(solution)/shard_map/psum | solution.py:52
  142.2 0.1 constant_dynamic-update-slice_fusion.20
  142.3 4.1 collective-permute-start.7
  146.4 1.9 collective-permute-start.6
  148.3 0.0 collective-permute-done.7
  148.3 5.1 collective-permute-done.6
  153.4 0.0 collective-permute-start.9
  153.4 1.7 collective-permute-start.8
  155.2 2.3 collective-permute-done.9
  157.5 0.0 collective-permute-done.8
  157.5 0.0 copy-start.4
  157.5 0.0 copy-start.5
  157.5 1.9 collective-permute-start.11
  159.5 5.1 collective-permute-start.10
  164.6 6.2 collective-permute-done.10
  170.8 0.0 collective-permute-done.11
  170.9 1.4 fusion.14
  172.3 97.8 %psum.44 = f32[32]{0:T(128)S(1)} all-reduce(f32[32]{0:T(128)S(1)} %get-tuple-element.16), channel_id=1, replica_groups=mesh['ta'=8,'gz'=8,'xy'=8] {'ta','gz','xy'}, use_global_device_ids=true, to_apply=%region_5.6 | all-reduce | flops 32 | bytes 256 | tf_op jit(solution)/shard_map/psum | solution.py:59
  270.1 0.2 multiply_reduce_fusion
  270.3 0.1 fusion.11
  270.5 94.5 %all-reduce = (f32[32]{0:T(128)S(1)}, f32[32]{0:T(128)S(1)}) all-reduce(f32[32]{0:T(128)S(1)} %fusion.11, f32[32]{0:T(128)S(1)} %get-tuple-element.6), channel_id=1, replica_groups=mesh['ta'=8,'gz'=8,'xy'=8] {'ta','gz','xy'}, use_global_device_ids=true, to_apply=%region_7.8 | all-reduce | flops 64 | bytes 512 | tf_op jit(solution)/shard_map/psum | solution.py:63
  364.9 0.1 bitcast_subtract_fusion
  365.0 0.0 copy-done.4
  365.0 0.0 copy-start.3
  365.0 0.2 fusion.8
  365.2 0.0 copy-done.5
  365.2 1.4 convolution_bitcast_fusion
  366.6 1.4 copy.19
  368.0 1.2 reshape.34
  369.2 0.0 copy-done.3
  369.2 0.0 all-reduce.4.cloned.1.call-update
  369.3 267.9 %all-reduce.4.cloned.1.call-done = f32[2048,32]{0,1:T(8,128)} async-done(((f32[2048,32]{0,1:T(8,128)}), f32[2048,32]{0,1:T(8,128)}) %all-reduce.4.cloned.1.call-update) | async-done | bytes 262160 | tf_op jit(solution)/shard_map/psum | solution.py:83
  637.2 0.0 copy-done
  637.2 2.9 convolution_bitcast_fusion.2
  640.1 26.9 %all_gather.3 = f32[2048,32]{0,1:T(8,128)} all-gather(f32[256,32]{0,1:T(8,128)S(1)} %convolution_bitcast_fusion.2), channel_id=1, replica_groups=mesh['ta'=8,'gz'=8,'xy'=8] {'xy'}, dimensions={0}, use_global_device_ids=true | all-gather | bytes 294912 | tf_op jit(solution)/shard_map/all_gather | solution.py:90
  667.0 1.3 reshape.35
  668.2 1.2 copy.24
  669.5 2.2 fusion.17
  671.6 0.9 fusion.5
  (25 shorter events, 0.1 us)
Async XLA Ops:
  7.2 630.0 %copy-start = (f32[256,2048]{1,0:T(8,128)S(1)}, f32[256,2048]{1,0:T(8,128)}, u32[]{:S(2)}) copy-start(f32[256,2048]{1,0:T(8,128)} %param.9) | copy-start | bytes 6291460
  7.2 36.0 %copy-start.2 = (f32[1,1,1,2,32,128]{5,4,3,2,1,0:T(8,128)S(1)}, f32[1,1,1,2,32,128]{5,4,3,2,1,0:T(8,128)}, u32[]{:S(2)}) copy-start(f32[1,1,1,2,32,128]{5,4,3,2,1,0:T(8,128)} %param.5) | copy-start | bytes 98308
  7.2 36.0 %copy-start.1 = (f32[1,1,1,2,9,128,128]{6,5,4,3,2,1,0:T(8,128)S(1)}, f32[1,1,1,2,9,128,128]{6,5,4,3,2,1,0:T(8,128)}, u32[]{:S(2)}) copy-start(f32[1,1,1,2,9,128,128]{6,5,4,3,2,1,0:T(8,128)} %param.6) | copy-start | bytes 3538948
  7.2 630.0 %all-reduce.4.cloned.1.call-start = ((), (), s32[]{:S(2)}) async-start(), calls=%async_computation | async-start | bytes 524288 | tf_op jit(solution)/shard_map/psum | solution.py:83
  7.2 8.4 %collective-permute-start.1 = (f32[1,1,1,2,32,128]{5,4,3,2,1,0:T(8,128)}, f32[1,1,1,2,32,128]{5,4,3,2,1,0:T(8,128)S(1)}, u32[]{:S(2)}, u32[]{:S(2)}) collective-permute-start(f32[1,1,1,2,32,128]{5,4,3,2,1,0:T(8,128)} %param.5), channel_id=1, source_target_pairs={{0,64},{64,128},{128,192},{192,256},{256,320},{320,384},{384,448},... | collective-permute-start | bytes 98312 | tf_op jit(solution)/shard_map/ppermute | solution.py:14
  12.2 7.2 %collective-permute-start = (f32[1,1,1,2,32,128]{5,4,3,2,1,0:T(8,128)}, f32[1,1,1,2,32,128]{5,4,3,2,1,0:T(8,128)S(1)}, u32[]{:S(2)}, u32[]{:S(2)}) collective-permute-start(f32[1,1,1,2,32,128]{5,4,3,2,1,0:T(8,128)} %param.5), channel_id=1, source_target_pairs={{64,0},{128,64},{192,128},{256,192},{320,256},{384,320},{448,384},... | collective-permute-start | bytes 98312 | tf_op jit(solution)/shard_map/ppermute | solution.py:16
  19.5 4.0 collective-permute-start.3
  19.5 4.0 collective-permute-start.2
  23.5 19.6 %collective-permute-start.5 = (f32[3,3,1,2,32,128]{5,4,3,2,1,0:T(8,128)S(1)}, f32[3,3,1,2,32,128]{5,4,3,2,1,0:T(8,128)S(1)}, u32[]{:S(2)}, u32[]{:S(2)}) collective-permute-start(f32[3,3,1,2,32,128]{5,4,3,2,1,0:T(8,128)S(1)} %pad_maximum_fusion), channel_id=1, source_target_pairs={{0,1},{1,2},{2,3},{3,4},{4,5},{5,6},{6,7},{7,0},{8,9},{9,10},{10,1... | collective-permute-start | bytes 884744 | tf_op jit(solution)/shard_map/ppermute | solution.py:14
  27.8 15.3 %collective-permute-start.4 = (f32[3,3,1,2,32,128]{5,4,3,2,1,0:T(8,128)S(1)}, f32[3,3,1,2,32,128]{5,4,3,2,1,0:T(8,128)S(1)}, u32[]{:S(2)}, u32[]{:S(2)}) collective-permute-start(f32[3,3,1,2,32,128]{5,4,3,2,1,0:T(8,128)S(1)} %pad_maximum_fusion), channel_id=1, source_target_pairs={{1,0},{2,1},{3,2},{4,3},{5,4},{6,5},{7,6},{0,7},{9,8},{10,9},{11,1... | collective-permute-start | bytes 884744 | tf_op jit(solution)/shard_map/ppermute | solution.py:16
  142.3 6.0 collective-permute-start.7
  146.4 7.0 %collective-permute-start.6 = (f32[1,1,1,2,32,128]{5,4,3,2,1,0:T(8,128)S(1)}, f32[1,1,1,2,32,128]{5,4,3,2,1,0:T(8,128)S(1)}, u32[]{:S(2)}, u32[]{:S(2)}) collective-permute-start(f32[1,1,1,2,32,128]{5,4,3,2,1,0:T(8,128)S(1)} %get-tuple-element.9), channel_id=1, source_target_pairs={{64,0},{128,64},{192,128},{256,192},{320,256},{384,320},{448,384},... | collective-permute-start | bytes 98312 | tf_op jit(solution)/shard_map/ppermute | solution.py:16
  153.4 4.1 collective-permute-start.9
  153.4 4.0 collective-permute-start.8
  157.5 207.5 %copy-start.4 = (f32[1,1,1,2,32,128]{5,4,3,2,1,0:T(8,128)S(1)}, f32[1,1,1,2,32,128]{5,4,3,2,1,0:T(8,128)}, u32[]{:S(2)}) copy-start(f32[1,1,1,2,32,128]{5,4,3,2,1,0:T(8,128)} %param.7) | copy-start | bytes 98308
  157.5 207.7 %copy-start.5 = (s32[1,1,1,2]{3,2,1,0:T(1,128)S(1)}, s32[1,1,1,2]{3,2,1,0:T(1,128)}, u32[]{:S(2)}) copy-start(s32[1,1,1,2]{3,2,1,0:T(1,128)} %param.8) | copy-start | bytes 28
  157.5 13.3 %collective-permute-start.11 = (f32[3,3,1,2,32,128]{5,4,3,2,1,0:T(8,128)S(1)}, f32[3,3,1,2,32,128]{5,4,3,2,1,0:T(8,128)S(1)}, u32[]{:S(2)}, u32[]{:S(2)}) collective-permute-start(f32[3,3,1,2,32,128]{5,4,3,2,1,0:T(8,128)S(1)} %pad_maximum_fusion.1), channel_id=1, source_target_pairs={{0,1},{1,2},{2,3},{3,4},{4,5},{5,6},{6,7},{7,0},{8,9},{9,10},{10,1... | collective-permute-start | bytes 884744 | tf_op jit(solution)/shard_map/ppermute | solution.py:14
  159.5 11.4 %collective-permute-start.10 = (f32[3,3,1,2,32,128]{5,4,3,2,1,0:T(8,128)S(1)}, f32[3,3,1,2,32,128]{5,4,3,2,1,0:T(8,128)S(1)}, u32[]{:S(2)}, u32[]{:S(2)}) collective-permute-start(f32[3,3,1,2,32,128]{5,4,3,2,1,0:T(8,128)S(1)} %pad_maximum_fusion.1), channel_id=1, source_target_pairs={{1,0},{2,1},{3,2},{4,3},{5,4},{6,5},{7,6},{0,7},{9,8},{10,9},{11,1... | collective-permute-start | bytes 884744 | tf_op jit(solution)/shard_map/ppermute | solution.py:16
  365.0 4.2 copy-start.3
Sparse Core Ops, SparseCore 0:
  369.4 267.7 all-reduce.3
where the time goes:
time: 680 us; the launch traced here: 679 us
  blocking collectives  317 us (47%)
  waiting for transfers between devices  294 us (43%)
  starting transfers between devices  36.3 us (5%)
  between operations  14.3 us (2%)
  matrix products  10.4 us (2%)
  local copies, waits for them, and re-layouts  7.46 us (1%)
    psum x1, waiting for transfers between devices, body(): coarse_rhs = lax.psum(partial_rhs, ('ta', 'gz', 'xy'))  268 us
    psum x1, blocking collectives, body(): lax.psum(inner_sum(image_first, image_raw), ('ta', 'gz', 'xy'))  97.8 us
    psum x1, blocking collectives, body(): lax.psum((inner_sum(image_first, right_side), inner_sum(image_first, imag...  97.5 us
    psum x1, blocking collectives, body(): lax.psum((inner_sum(image_second, resid_mid), inner_sum(image_second, ima...  94.5 us
    all_gather x1, blocking collectives, body(): correction = lax.all_gather(rows_part, 'xy', axis=0, tiled=True)  26.9 us
    ppermute x6, starting transfers between devices, extended(): lax.ppermute(head, axis, [((i + 1) % count, i) for i in range(count)])  21 us
    ppermute x6, waiting for transfers between devices, extended(): lax.ppermute(head, axis, [((i + 1) % count, i) for i in range(count)])  21 us
    ppermute x6, starting transfers between devices, extended(): lax.ppermute(tail, axis, [(i, (i + 1) % count) for i in range(count)])  15.2 us
  transfers between devices with their start and end apart: 13, of which 7 were waited for; matrix products, arithmetic and copies ran while one was open for 0% of the time, Pallas kernels for 0%

commit v1 on v0

--- a/solution.py
+++ b/solution.py
@@ -56,7 +56,9 @@
     step_first = cross_first / square_first
     resid_mid = right_side - step_first[:, None] * image_first
     image_raw = apply_operator(resid_mid, stencil)
-    correlation_sum = lax.psum(inner_sum(image_first, image_raw), ("ta", "gz", "xy"))
+    correlation_sum = jnp.sum(
+        lax.all_gather(inner_sum(image_first, image_raw), ("ta", "gz", "xy")), axis=0
+    )
     beta = correlation_sum / square_first
     image_second = image_raw - beta[:, None] * image_first
     direction = resid_mid - beta[:, None] * right_side

time: 680 us -> 845 us (1.24)
  waiting for transfers between devices: 294 us -> 546 us
  blocking collectives: 317 us -> 221 us
    unnamed x1 -> x3, waiting for transfers between devices: 0.02 us -> 257 us
    psum x1 -> x0, blocking collectives: 97.8 us -> none  [body(): lax.psum(inner_sum(image_first, image_raw), ('ta', 'gz', 'xy'))]
  transfers between devices with their start and end apart: 13 -> 14, of which waited for: 7 -> 8; matrix products, arithmetic and copies ran while one was open for 0% -> 1% of each run, Pallas kernels for 0% -> 0%
where the time goes in v1:
time: 845 us; the launch traced here: 844 us
  waiting for transfers between devices  546 us (65%)
  blocking collectives  221 us (26%)
  starting transfers between devices  36.4 us (4%)
  between operations  14.3 us (2%)
  local copies, waits for them, and re-layouts  13.6 us (2%)
  matrix products  11.4 us (1%)
    psum x1, waiting for transfers between devices, body(): coarse_rhs = lax.psum(partial_rhs, ('ta', 'gz', 'xy'))  266 us
    unnamed x3, waiting for transfers between devices  257 us
    psum x1, blocking collectives, body(): lax.psum((inner_sum(image_first, right_side), inner_sum(image_first, imag...  97.5 us
    psum x1, blocking collectives, body(): lax.psum((inner_sum(image_second, resid_mid), inner_sum(image_second, ima...  96.6 us
    all_gather x1, blocking collectives, body(): correction = lax.all_gather(rows_part, 'xy', axis=0, tiled=True)  26.9 us
    ppermute x6, starting transfers between devices, extended(): lax.ppermute(head, axis, [((i + 1) % count, i) for i in range(count)])  21 us
    ppermute x6, waiting for transfers between devices, extended(): lax.ppermute(head, axis, [((i + 1) % count, i) for i in range(count)])  19.2 us
  transfers between devices with their start and end apart: 14, of which 8 were waited for; matrix products, arithmetic and copies ran while one was open for 1% of the time, Pallas kernels for 0%

profile of v1, /device:TPU:26, one launch (start us, length us, event | category | flops | bytes accessed | tf_op | source)
XLA Modules:
  0.0 844.1 jit_solution(17492289732740257554)
XLA Ops:
  7.2 0.0 copy-start
  7.2 0.0 copy-start.2
  7.2 0.0 all-reduce.8.cloned.1.call-start
  7.2 5.0 collective-permute-start.1
  12.2 1.9 collective-permute-start
  14.1 1.4 constant_dynamic-update-slice_fusion.11
  15.5 0.7 slice_bitcast_fusion.11
  16.3 0.0 collective-permute-done.1
  16.3 0.8 constant_dynamic-update-slice_fusion.1
  17.0 2.4 collective-permute-done
  19.5 0.0 collective-permute-start.3
  19.5 1.7 collective-permute-start.2
  21.2 0.6 constant_dynamic-update-slice_fusion.10
  21.8 0.6 constant_dynamic-update-slice_fusion.9
  22.4 1.1 collective-permute-done.3
  23.5 4.3 collective-permute-start.5
  27.8 8.6 %collective-permute-start.4 = (f32[3,3,1,2,32,128]{5,4,3,2,1,0:T(8,128)S(1)}, f32[3,3,1,2,32,128]{5,4,3,2,1,0:T(8,128)S(1)}, u32[]{:S(2)}, u32[]{:S(2)}) collective-permute-start(f32[3,3,1,2,32,128]{5,4,3,2,1,0:T(8,128)S(1)} %pad_maximum_fusion), channel_id=1, source_target_pairs={{1,0},{2,1},{3,2},{4,3},{5,4},{6,5},{7,6},{0,7},{9,8},{10,9},{11,1... | collective-permute-start | bytes 884744 | tf_op jit(solution)/shard_map/ppermute | solution.py:16
  36.4 0.6 constant_dynamic-update-slice_fusion.8
  37.0 0.6 constant_dynamic-update-slice_fusion.7
  37.6 5.5 collective-permute-done.4
  43.1 0.6 constant_dynamic-update-slice_fusion.6
  43.8 0.6 constant_dynamic-update-slice_fusion.5
  44.4 0.6 constant_dynamic-update-slice_fusion.4
  45.0 0.6 constant_dynamic-update-slice_fusion.3
  45.6 2.4 fusion.6
  48.0 0.1 fusion.13
  48.1 97.5 %all-reduce.2 = (f32[32]{0:T(128)S(1)}, f32[32]{0:T(128)S(1)}) all-reduce(f32[32]{0:T(128)S(1)} %get-tuple-element.14, f32[32]{0:T(128)S(1)} %fusion.13), channel_id=1, replica_groups=mesh['ta'=8,'gz'=8,'xy'=8] {'ta','gz','xy'}, use_global_device_ids=true, to_apply=%region_1.2 | all-reduce | flops 64 | bytes 512 | tf_op jit(solution)/shard_map/psum | solution.py:52
  145.6 0.1 constant_dynamic-update-slice_fusion.20
  145.7 4.1 collective-permute-start.7
  149.7 1.9 collective-permute-start.6
  151.7 0.0 collective-permute-done.7
  151.7 5.1 collective-permute-done.6
  156.8 0.0 collective-permute-start.9
  156.8 1.7 collective-permute-start.8
  158.5 2.3 collective-permute-done.9
  160.9 1.9 collective-permute-start.11
  162.8 5.1 collective-permute-start.10
  167.9 6.2 collective-permute-done.10
  174.2 0.0 copy-start.5
  174.2 0.0 copy-start.6
  174.2 1.4 fusion.14
  175.7 0.3 dynamic-update-slice
  176.0 0.6 copy-done.3
  176.6 0.0 all-reduce.8.cloned.1.call-update
  176.6 0.0 all-reduce.6.cloned.1.call-start
  176.6 256.7 %all-reduce.8.cloned.1.call-done = f32[16384]{0:T(1024)} async-done(((f32[16384]{0:T(1024)}), f32[16384]{0:T(1024)}) %all-reduce.8.cloned.1.call-update) | async-done | bytes 65552
  433.4 0.9 reshape.36
  434.3 0.1 reduce_sum.57
  434.4 0.2 multiply_reduce_fusion
  434.6 0.1 fusion.11
  434.7 96.6 %all-reduce.1 = (f32[32]{0:T(128)S(1)}, f32[32]{0:T(128)S(1)}) all-reduce(f32[32]{0:T(128)S(1)} %fusion.11, f32[32]{0:T(128)S(1)} %get-tuple-element.6), channel_id=1, replica_groups=mesh['ta'=8,'gz'=8,'xy'=8] {'ta','gz','xy'}, use_global_device_ids=true, to_apply=%region_7.8 | all-reduce | flops 64 | bytes 512 | tf_op jit(solution)/shard_map/psum | solution.py:65
  531.3 0.1 bitcast_subtract_fusion
  531.4 0.2 fusion.8
  531.6 1.4 convolution_bitcast_fusion
  533.0 1.4 copy.19
  534.4 1.2 reshape.34
  535.6 0.0 all-reduce.6.cloned.1.call-update
  535.6 266.4 %all-reduce.6.cloned.1.call-done = f32[2048,32]{0,1:T(8,128)} async-done(((f32[2048,32]{0,1:T(8,128)}), f32[2048,32]{0,1:T(8,128)}) %all-reduce.6.cloned.1.call-update) | async-done | bytes 262160 | tf_op jit(solution)/shard_map/psum | solution.py:85
  802.0 2.9 convolution_bitcast_fusion.2
  804.9 26.9 %all_gather.11 = f32[2048,32]{0,1:T(8,128)} all-gather(f32[256,32]{0,1:T(8,128)S(1)} %convolution_bitcast_fusion.2), channel_id=1, replica_groups=mesh['ta'=8,'gz'=8,'xy'=8] {'xy'}, dimensions={0}, use_global_device_ids=true | all-gather | bytes 294912 | tf_op jit(solution)/shard_map/all_gather | solution.py:92
  831.8 1.3 reshape.35
  833.0 1.2 copy.24
  834.3 2.2 fusion.17
  836.4 0.9 fusion.5
  (31 shorter events, 0.1 us)
Async XLA Ops:
  7.2 794.8 %copy-start = (f32[256,2048]{1,0:T(8,128)S(1)}, f32[256,2048]{1,0:T(8,128)}, u32[]{:S(2)}) copy-start(f32[256,2048]{1,0:T(8,128)} %param.9) | copy-start | bytes 6291460
  7.2 38.4 %copy-start.2 = (f32[1,1,1,2,32,128]{5,4,3,2,1,0:T(8,128)S(1)}, f32[1,1,1,2,32,128]{5,4,3,2,1,0:T(8,128)}, u32[]{:S(2)}) copy-start(f32[1,1,1,2,32,128]{5,4,3,2,1,0:T(8,128)} %param.5) | copy-start | bytes 98308
  7.2 38.4 %copy-start.1 = (f32[1,1,1,2,9,128,128]{6,5,4,3,2,1,0:T(8,128)S(1)}, f32[1,1,1,2,9,128,128]{6,5,4,3,2,1,0:T(8,128)}, u32[]{:S(2)}) copy-start(f32[1,1,1,2,9,128,128]{6,5,4,3,2,1,0:T(8,128)} %param.6) | copy-start | bytes 3538948
  7.2 426.2 %all-reduce.8.cloned.1.call-start = ((), (), s32[]{:S(2)}) async-start(), calls=%async_computation.1 | async-start | bytes 131072
  7.2 9.0 %collective-permute-start.1 = (f32[1,1,1,2,32,128]{5,4,3,2,1,0:T(8,128)}, f32[1,1,1,2,32,128]{5,4,3,2,1,0:T(8,128)S(1)}, u32[]{:S(2)}, u32[]{:S(2)}) collective-permute-start(f32[1,1,1,2,32,128]{5,4,3,2,1,0:T(8,128)} %param.5), channel_id=1, source_target_pairs={{0,64},{64,128},{128,192},{192,256},{256,320},{320,384},{384,448},... | collective-permute-start | bytes 98312 | tf_op jit(solution)/shard_map/ppermute | solution.py:14
  12.2 7.2 collective-permute-start
  19.5 4.0 collective-permute-start.3
  19.5 4.0 collective-permute-start.2
  23.5 20.2 %collective-permute-start.5 = (f32[3,3,1,2,32,128]{5,4,3,2,1,0:T(8,128)S(1)}, f32[3,3,1,2,32,128]{5,4,3,2,1,0:T(8,128)S(1)}, u32[]{:S(2)}, u32[]{:S(2)}) collective-permute-start(f32[3,3,1,2,32,128]{5,4,3,2,1,0:T(8,128)S(1)} %pad_maximum_fusion), channel_id=1, source_target_pairs={{0,1},{1,2},{2,3},{3,4},{4,5},{5,6},{6,7},{7,0},{8,9},{9,10},{10,1... | collective-permute-start | bytes 884744 | tf_op jit(solution)/shard_map/ppermute | solution.py:14
  27.8 15.3 %collective-permute-start.4 = (f32[3,3,1,2,32,128]{5,4,3,2,1,0:T(8,128)S(1)}, f32[3,3,1,2,32,128]{5,4,3,2,1,0:T(8,128)S(1)}, u32[]{:S(2)}, u32[]{:S(2)}) collective-permute-start(f32[3,3,1,2,32,128]{5,4,3,2,1,0:T(8,128)S(1)} %pad_maximum_fusion), channel_id=1, source_target_pairs={{1,0},{2,1},{3,2},{4,3},{5,4},{6,5},{7,6},{0,7},{9,8},{10,9},{11,1... | collective-permute-start | bytes 884744 | tf_op jit(solution)/shard_map/ppermute | solution.py:16
  145.7 6.0 collective-permute-start.7
  149.7 7.0 collective-permute-start.6
  156.8 4.1 collective-permute-start.9
  156.8 4.0 collective-permute-start.8
  160.9 13.3 %collective-permute-start.11 = (f32[3,3,1,2,32,128]{5,4,3,2,1,0:T(8,128)S(1)}, f32[3,3,1,2,32,128]{5,4,3,2,1,0:T(8,128)S(1)}, u32[]{:S(2)}, u32[]{:S(2)}) collective-permute-start(f32[3,3,1,2,32,128]{5,4,3,2,1,0:T(8,128)S(1)} %pad_maximum_fusion.1), channel_id=1, source_target_pairs={{0,1},{1,2},{2,3},{3,4},{4,5},{5,6},{6,7},{7,0},{8,9},{9,10},{10,1... | collective-permute-start | bytes 884744 | tf_op jit(solution)/shard_map/ppermute | solution.py:14
  162.8 11.4 %collective-permute-start.10 = (f32[3,3,1,2,32,128]{5,4,3,2,1,0:T(8,128)S(1)}, f32[3,3,1,2,32,128]{5,4,3,2,1,0:T(8,128)S(1)}, u32[]{:S(2)}, u32[]{:S(2)}) collective-permute-start(f32[3,3,1,2,32,128]{5,4,3,2,1,0:T(8,128)S(1)} %pad_maximum_fusion.1), channel_id=1, source_target_pairs={{1,0},{2,1},{3,2},{4,3},{5,4},{6,5},{7,6},{0,7},{9,8},{10,9},{11,1... | collective-permute-start | bytes 884744 | tf_op jit(solution)/shard_map/ppermute | solution.py:16
  174.2 357.2 %copy-start.5 = (f32[1,1,1,2,32,128]{5,4,3,2,1,0:T(8,128)S(1)}, f32[1,1,1,2,32,128]{5,4,3,2,1,0:T(8,128)}, u32[]{:S(2)}) copy-start(f32[1,1,1,2,32,128]{5,4,3,2,1,0:T(8,128)} %param.7) | copy-start | bytes 98308
  174.2 357.3 %copy-start.6 = (s32[1,1,1,2]{3,2,1,0:T(1,128)S(1)}, s32[1,1,1,2]{3,2,1,0:T(1,128)}, u32[]{:S(2)}) copy-start(s32[1,1,1,2]{3,2,1,0:T(1,128)} %param.8) | copy-start | bytes 28
  176.0 0.6 copy-start.3
  176.6 625.4 %all-reduce.6.cloned.1.call-start = ((), (), s32[]{:S(2)}) async-start(), calls=%async_computation | async-start | bytes 524288 | tf_op jit(solution)/shard_map/psum | solution.py:85
  531.4 4.2 copy-start.4
Sparse Core Ops, SparseCore 0:
  176.7 256.6 all-reduce.7
  535.7 266.2 all-reduce.5
